TPU v7x, 32 devices: a whole 2x2x4 slice. The times are simulated.
32 devices in a mesh: blk: 4 (over z), grp: 8 (over y, x, core).
Axes of the slice: x: 2, y: 2, z: 4, core: 2. Of those that a mesh axis runs over, the one named last changes fastest.
Arguments:
- position: float32 [3, 16384], P(None, ('blk', 'grp')), may hold values from -6 to 6
- velocity: float32 [3, 16384], P(None, ('blk', 'grp')), may hold values from -6 to 6
- accel_old: float32 [3, 16384], P(None, ('blk', 'grp')), may hold values from -6 to 6
- jerk_old: float32 [3, 16384], P(None, ('blk', 'grp')), may hold values from -6 to 6
- mass: float32 [16384], P(('blk', 'grp')), may hold values from 1e-07 to 1e-05
- elapsed: float32 [16384], P(('blk', 'grp')), may hold values from 0.1 to 1
- active_index: int32 [512], P(('blk', 'grp')), may hold values from 0 to 16383, as said below
Outputs:
- predicted: float32 [6, 16384], P(None, ('blk', 'grp'))
- accel: float32 [3, 512], P(None, ('blk', 'grp'))
- jerk: float32 [3, 512], P(None, ('blk', 'grp'))
Inputs may be any that keep to these rules, and one draw needn't show every extreme that they name: `active_index`: entries 16 * k to 16 * k + 15 are distinct stars of the range 512 * k to 512 * k + 511, for every k.
All inputs are finite; a program needn't handle non-finite values.
Results may differ from a plain program's by a relative error of at most 0.0003.
Values sent between devices are 32-bit elements; how exact they have to be, the bound alone decides.
A program may use at most 64 MiB of HBM per device.

v0:
```python
import math
import jax
import jax.numpy as jnp
from jax import lax
from jax.sharding import PartitionSpec as P

SOFTENING = 0.0001


def from_behind(shard, axis, by):
    count = lax.axis_size(axis)
    return lax.ppermute(shard, axis, [(i, (i + by) % count) for i in range(count)])


def predict(position, velocity, accel_old, jerk_old, elapsed):
    step_row = elapsed[None, :]
    half = step_row * step_row * 0.5
    sixth = half * step_row * (1.0 / 3.0)
    new_position = position + step_row * velocity + half * accel_old + sixth * jerk_old
    new_velocity = velocity + step_row * accel_old + half * jerk_old
    return jnp.concatenate([new_position, new_velocity], 0)


def interact(targets, sources, masses):
    columns = targets.shape[1]
    block_size = math.gcd(columns, 128)
    blocks = columns // block_size
    stacked = targets.reshape(6, blocks, block_size).transpose(1, 0, 2)

    def one_block(target_block):
        separation = sources[0:3][:, None, :] - target_block[0:3][:, :, None]
        relative = sources[3:6][:, None, :] - target_block[3:6][:, :, None]
        distance = jnp.sum(separation * separation, 0) + SOFTENING
        inverse = 1.0 / jnp.sqrt(distance)
        weight = masses[None, :] * inverse * inverse * inverse
        radial = 3.0 * jnp.sum(separation * relative, 0) / distance
        accel_part = jnp.sum(weight[None] * separation, 2)
        jerk_part = jnp.sum(weight[None] * (relative - radial[None] * separation), 2)
        return jnp.concatenate([accel_part, jerk_part], 0)

    result = lax.map(one_block, stacked)
    return result.transpose(1, 0, 2).reshape(6, columns)


def local(position, velocity, accel_old, jerk_old, mass, elapsed, active_index):
    predicted = predict(position, velocity, accel_old, jerk_old, elapsed)
    stars_here = position.shape[1]
    device = lax.axis_index("blk") * lax.axis_size("grp") + lax.axis_index("grp")
    offsets = active_index - device * stars_here
    owned_rows = jnp.take(predicted, offsets, axis=1)
    group_rows = lax.all_gather(owned_rows, "grp", axis=1, tiled=True)

    def circulate(number, carry):
        visitor, partial_value = carry
        partial_value = partial_value + interact(visitor, predicted, mass)
        return from_behind((visitor, partial_value), "blk", 1)

    start = jnp.zeros(group_rows.shape, jnp.float32)
    visitor, partial_value = lax.fori_loop(0, lax.axis_size("blk"), circulate, (group_rows, start))
    owned = lax.psum_scatter(partial_value, "grp", scatter_dimension=1, tiled=True)
    return (predicted, owned[0:3], owned[3:6])


def solution(mesh):
    in_specs = (
        P(None, ("blk", "grp")),
        P(None, ("blk", "grp")),
        P(None, ("blk", "grp")),
        P(None, ("blk", "grp")),
        P(("blk", "grp")),
        P(("blk", "grp")),
        P(("blk", "grp")),
    )
    out_specs = (P(None, ("blk", "grp")), P(None, ("blk", "grp")), P(None, ("blk", "grp")))
    return jax.shard_map(local, mesh=mesh, in_specs=in_specs, out_specs=out_specs, check_vma=False)
```

profile of v0, /device:TPU:0, one launch (start us, length us, event | category | flops | bytes accessed | tf_op | source)
XLA Modules:
  0.0 89.8 jit_solution(8160792300937886255)
XLA Ops:
  7.2 0.0 reduce-scatter.4.cloned.1.call-start
  7.2 0.0 copy-start.6
  7.2 0.0 copy-start.5
  7.2 0.0 copy-start.7
  7.2 0.0 copy-start.4
  7.3 0.6 copy-done.7
  7.9 0.0 copy-start.2
  7.9 0.0 copy-start.3
  7.9 0.7 copy-done.2
  8.6 0.0 copy-done.6
  8.6 0.0 copy-done.5
  8.6 0.0 copy-done.4
  8.6 0.0 copy-done.3
  8.7 0.0 copy-start
  8.7 0.1 copy.46
  8.8 0.4 copy-done
  9.3 0.6 gather_fusion
  9.8 0.1 broadcast_select_fusion
  9.9 0.1 copy.47
  10.0 10.6 %all-gather = f32[8,16,6]{1,2,0:T(8,128)S(1)} all-gather(f32[1,16,6]{1,2,0:T(8,128)S(1)} %bitcast.9), channel_id=1, replica_groups=mesh['blk'=4,'grp'=8] {'grp'}, dimensions={0}, use_global_device_ids=true | all-gather | bytes 3456 | tf_op jit(solution)/shard_map/all_gather | solution.py:51
  20.6 0.1 reshape.66
  20.7 0.0 copy-start.1
  20.7 0.7 copy-done.1
  21.3 26.4 %while.11 = (s32[]{:T(128)}, f32[6,128]{1,0:T(8,128)S(1)}, f32[6,128]{1,0:T(8,128)S(1)}, f32[3,512]{1,0:T(4,128)S(1)}, f32[512]{0:T(512)S(1)}, /*index=5*/f32[3,512]{1,0:T(4,128)S(1)}, s32[]{:T(128)}) while((s32[]{:T(128)}, f32[6,128]{1,0:T(8,128)S(1)}, f32[6,128]{1,0:T(8,128)S(1)}, f32[3,512]{1,0:T(4,128)S(1)}, f32[512]{0:T(512)S(1)}, ...), condition=%wide.region_5.6_spmd, body=%wide.region_0.5_spmd.sunk | while | flops 3015426 | bytes 2179229 | solution.py:59
  21.3 1.6 %collective-permute-start = (f32[6,128]{1,0:T(8,128)S(1)}, f32[6,128]{1,0:T(8,128)S(1)}, u32[]{:S(2)}, u32[]{:S(2)}) collective-permute-start(f32[6,128]{1,0:T(8,128)S(1)} %copy.57), channel_id=1, source_target_pairs={{0,8},{8,16},{16,24},{24,0},{1,9},{9,17},{17,25},{25,1},{2,10},{10... | collective-permute-start | bytes 9224 | tf_op jit(solution)/shard_map/while/body/eval_jaxpr/ppermute | solution.py:12
  22.9 0.2 fusion.11
  23.1 0.1 multiply_divide_fusion.2
  23.2 0.4 fusion.12
  23.6 1.6 %collective-permute-start.1 = (f32[6,128]{1,0:T(8,128)S(1)}, f32[6,128]{1,0:T(8,128)S(1)}, u32[]{:S(2)}, u32[]{:S(2)}) collective-permute-start(f32[6,128]{1,0:T(8,128)S(1)} %maximum_add_fusion.2), channel_id=1, source_target_pairs={{0,8},{8,16},{16,24},{24,0},{1,9},{9,17},{17,25},{25,1},{2,10},{10... | collective-permute-start | bytes 9224 | tf_op jit(solution)/shard_map/while/body/eval_jaxpr/ppermute | solution.py:12
  25.3 1.5 %collective-permute-done = f32[6,128]{1,0:T(8,128)S(1)} collective-permute-done((f32[6,128]{1,0:T(8,128)S(1)}, f32[6,128]{1,0:T(8,128)S(1)}, u32[]{:S(2)}, u32[]{:S(2)}) %collective-permute-start) | collective-permute-done | bytes 3104 | tf_op jit(solution)/shard_map/while/body/eval_jaxpr/ppermute | solution.py:12
  26.7 2.4 %collective-permute-done.1 = f32[6,128]{1,0:T(8,128)S(1)} collective-permute-done((f32[6,128]{1,0:T(8,128)S(1)}, f32[6,128]{1,0:T(8,128)S(1)}, u32[]{:S(2)}, u32[]{:S(2)}) %collective-permute-start.1) | collective-permute-done | bytes 3104 | tf_op jit(solution)/shard_map/while/body/eval_jaxpr/ppermute | solution.py:12
  29.1 0.0 collective-permute-start
  29.1 0.2 fusion.11
  29.3 0.1 multiply_divide_fusion.2
  29.4 0.4 fusion.12
  29.8 1.4 %collective-permute-start.1 = (f32[6,128]{1,0:T(8,128)S(1)}, f32[6,128]{1,0:T(8,128)S(1)}, u32[]{:S(2)}, u32[]{:S(2)}) collective-permute-start(f32[6,128]{1,0:T(8,128)S(1)} %maximum_add_fusion.2), channel_id=1, source_target_pairs={{0,8},{8,16},{16,24},{24,0},{1,9},{9,17},{17,25},{25,1},{2,10},{10... | collective-permute-start | bytes 9224 | tf_op jit(solution)/shard_map/while/body/eval_jaxpr/ppermute | solution.py:12
  31.2 3.3 %collective-permute-done = f32[6,128]{1,0:T(8,128)S(1)} collective-permute-done((f32[6,128]{1,0:T(8,128)S(1)}, f32[6,128]{1,0:T(8,128)S(1)}, u32[]{:S(2)}, u32[]{:S(2)}) %collective-permute-start) | collective-permute-done | bytes 3104 | tf_op jit(solution)/shard_map/while/body/eval_jaxpr/ppermute | solution.py:12
  34.5 0.8 collective-permute-done.1
  35.3 0.0 collective-permute-start
  35.3 0.2 fusion.11
  35.5 0.1 multiply_divide_fusion.2
  35.6 0.4 fusion.12
  36.0 0.9 %collective-permute-start.1 = (f32[6,128]{1,0:T(8,128)S(1)}, f32[6,128]{1,0:T(8,128)S(1)}, u32[]{:S(2)}, u32[]{:S(2)}) collective-permute-start(f32[6,128]{1,0:T(8,128)S(1)} %maximum_add_fusion.2), channel_id=1, source_target_pairs={{0,8},{8,16},{16,24},{24,0},{1,9},{9,17},{17,25},{25,1},{2,10},{10... | collective-permute-start | bytes 9224 | tf_op jit(solution)/shard_map/while/body/eval_jaxpr/ppermute | solution.py:12
  37.0 3.8 %collective-permute-done = f32[6,128]{1,0:T(8,128)S(1)} collective-permute-done((f32[6,128]{1,0:T(8,128)S(1)}, f32[6,128]{1,0:T(8,128)S(1)}, u32[]{:S(2)}, u32[]{:S(2)}) %collective-permute-start) | collective-permute-done | bytes 3104 | tf_op jit(solution)/shard_map/while/body/eval_jaxpr/ppermute | solution.py:12
  40.7 0.8 collective-permute-done.1
  41.5 0.0 collective-permute-start
  41.5 0.2 fusion.11
  41.7 0.1 multiply_divide_fusion.2
  41.8 0.4 fusion.12
  42.2 1.4 %collective-permute-start.1 = (f32[6,128]{1,0:T(8,128)S(1)}, f32[6,128]{1,0:T(8,128)S(1)}, u32[]{:S(2)}, u32[]{:S(2)}) collective-permute-start(f32[6,128]{1,0:T(8,128)S(1)} %maximum_add_fusion.2), channel_id=1, source_target_pairs={{0,8},{8,16},{16,24},{24,0},{1,9},{9,17},{17,25},{25,1},{2,10},{10... | collective-permute-start | bytes 9224 | tf_op jit(solution)/shard_map/while/body/eval_jaxpr/ppermute | solution.py:12
  43.6 3.3 %collective-permute-done = f32[6,128]{1,0:T(8,128)S(1)} collective-permute-done((f32[6,128]{1,0:T(8,128)S(1)}, f32[6,128]{1,0:T(8,128)S(1)}, u32[]{:S(2)}, u32[]{:S(2)}) %collective-permute-start) | collective-permute-done | bytes 3104 | tf_op jit(solution)/shard_map/while/body/eval_jaxpr/ppermute | solution.py:12
  46.9 0.8 collective-permute-done.1
  47.7 0.7 copy.49
  48.4 0.0 reduce-scatter.4.cloned.1.call-update
  48.5 32.4 %reduce-scatter.4.cloned.1.call-done = f32[16,6]{1,0:T(8,128)} async-done(((f32[128,6]{1,0:T(8,128)}), f32[16,6]{1,0:T(8,128)}) %reduce-scatter.4.cloned.1.call-update) | async-done | bytes 400
  80.8 0.8 fusion.6
  81.7 0.7 copy.52
  82.3 0.7 copy.51
  (19 shorter events, 0.1 us)
Async XLA Ops:
  7.2 73.7 %reduce-scatter.4.cloned.1.call-start = ((), (), s32[]{:S(2)}) async-start(), calls=%async_computation.1 | async-start | bytes 73728
  7.2 1.4 %copy-start.6 = (f32[3,512]{1,0:T(4,128)S(1)}, f32[3,512]{1,0:T(4,128)}, u32[]{:S(2)}) copy-start(f32[3,512]{1,0:T(4,128)} %param.10) | copy-start | bytes 18436
  7.2 1.4 %copy-start.5 = (f32[3,512]{1,0:T(4,128)S(1)}, f32[3,512]{1,0:T(4,128)}, u32[]{:S(2)}) copy-start(f32[3,512]{1,0:T(4,128)} %param.9) | copy-start | bytes 18436
  7.2 0.7 copy-start.7
  7.2 1.4 %copy-start.4 = (f32[3,512]{1,0:T(4,128)S(1)}, f32[3,512]{1,0:T(4,128)}, u32[]{:S(2)}) copy-start(f32[3,512]{1,0:T(4,128)} %param.11) | copy-start | bytes 18436
  7.9 0.7 copy-start.2
  7.9 0.7 copy-start.3
  8.7 0.6 copy-start
  20.7 0.7 copy-start.1
  21.3 5.4 %collective-permute-start = (f32[6,128]{1,0:T(8,128)S(1)}, f32[6,128]{1,0:T(8,128)S(1)}, u32[]{:S(2)}, u32[]{:S(2)}) collective-permute-start(f32[6,128]{1,0:T(8,128)S(1)} %copy.57), channel_id=1, source_target_pairs={{0,8},{8,16},{16,24},{24,0},{1,9},{9,17},{17,25},{25,1},{2,10},{10... | collective-permute-start | bytes 9224 | tf_op jit(solution)/shard_map/while/body/eval_jaxpr/ppermute | solution.py:12
  23.6 5.5 %collective-permute-start.1 = (f32[6,128]{1,0:T(8,128)S(1)}, f32[6,128]{1,0:T(8,128)S(1)}, u32[]{:S(2)}, u32[]{:S(2)}) collective-permute-start(f32[6,128]{1,0:T(8,128)S(1)} %maximum_add_fusion.2), channel_id=1, source_target_pairs={{0,8},{8,16},{16,24},{24,0},{1,9},{9,17},{17,25},{25,1},{2,10},{10... | collective-permute-start | bytes 9224 | tf_op jit(solution)/shard_map/while/body/eval_jaxpr/ppermute | solution.py:12
  29.1 5.4 %collective-permute-start = (f32[6,128]{1,0:T(8,128)S(1)}, f32[6,128]{1,0:T(8,128)S(1)}, u32[]{:S(2)}, u32[]{:S(2)}) collective-permute-start(f32[6,128]{1,0:T(8,128)S(1)} %copy.57), channel_id=1, source_target_pairs={{0,8},{8,16},{16,24},{24,0},{1,9},{9,17},{17,25},{25,1},{2,10},{10... | collective-permute-start | bytes 9224 | tf_op jit(solution)/shard_map/while/body/eval_jaxpr/ppermute | solution.py:12
  29.8 5.5 %collective-permute-start.1 = (f32[6,128]{1,0:T(8,128)S(1)}, f32[6,128]{1,0:T(8,128)S(1)}, u32[]{:S(2)}, u32[]{:S(2)}) collective-permute-start(f32[6,128]{1,0:T(8,128)S(1)} %maximum_add_fusion.2), channel_id=1, source_target_pairs={{0,8},{8,16},{16,24},{24,0},{1,9},{9,17},{17,25},{25,1},{2,10},{10... | collective-permute-start | bytes 9224 | tf_op jit(solution)/shard_map/while/body/eval_jaxpr/ppermute | solution.py:12
  35.3 5.4 %collective-permute-start = (f32[6,128]{1,0:T(8,128)S(1)}, f32[6,128]{1,0:T(8,128)S(1)}, u32[]{:S(2)}, u32[]{:S(2)}) collective-permute-start(f32[6,128]{1,0:T(8,128)S(1)} %copy.57), channel_id=1, source_target_pairs={{0,8},{8,16},{16,24},{24,0},{1,9},{9,17},{17,25},{25,1},{2,10},{10... | collective-permute-start | bytes 9224 | tf_op jit(solution)/shard_map/while/body/eval_jaxpr/ppermute | solution.py:12
  36.0 5.5 %collective-permute-start.1 = (f32[6,128]{1,0:T(8,128)S(1)}, f32[6,128]{1,0:T(8,128)S(1)}, u32[]{:S(2)}, u32[]{:S(2)}) collective-permute-start(f32[6,128]{1,0:T(8,128)S(1)} %maximum_add_fusion.2), channel_id=1, source_target_pairs={{0,8},{8,16},{16,24},{24,0},{1,9},{9,17},{17,25},{25,1},{2,10},{10... | collective-permute-start | bytes 9224 | tf_op jit(solution)/shard_map/while/body/eval_jaxpr/ppermute | solution.py:12
  41.5 5.4 %collective-permute-start = (f32[6,128]{1,0:T(8,128)S(1)}, f32[6,128]{1,0:T(8,128)S(1)}, u32[]{:S(2)}, u32[]{:S(2)}) collective-permute-start(f32[6,128]{1,0:T(8,128)S(1)} %copy.57), channel_id=1, source_target_pairs={{0,8},{8,16},{16,24},{24,0},{1,9},{9,17},{17,25},{25,1},{2,10},{10... | collective-permute-start | bytes 9224 | tf_op jit(solution)/shard_map/while/body/eval_jaxpr/ppermute | solution.py:12
  42.2 5.5 %collective-permute-start.1 = (f32[6,128]{1,0:T(8,128)S(1)}, f32[6,128]{1,0:T(8,128)S(1)}, u32[]{:S(2)}, u32[]{:S(2)}) collective-permute-start(f32[6,128]{1,0:T(8,128)S(1)} %maximum_add_fusion.2), channel_id=1, source_target_pairs={{0,8},{8,16},{16,24},{24,0},{1,9},{9,17},{17,25},{25,1},{2,10},{10... | collective-permute-start | bytes 9224 | tf_op jit(solution)/shard_map/while/body/eval_jaxpr/ppermute | solution.py:12
Sparse Core Ops, SparseCore 0:
  48.6 32.2 reduce-scatter.3
where the time goes:
time: 90.2 us; the launch traced here: 89.8 us
  waiting for transfers between devices  48.9 us (54%)
  between operations  14.1 us (16%)
  blocking collectives  10.6 us (12%)
  starting transfers between devices  6.96 us (8%)
  local copies, waits for them, and re-layouts  6.22 us (7%)
  other arithmetic  2.95 us (3%)
    unnamed x2, waiting for transfers between devices  32.4 us
    ppermute x8, waiting for transfers between devices, from_behind(): lax.ppermute(shard, axis, [(i, (i + by) % count) for i in range(count)])  16.5 us
    all_gather x1, blocking collectives, local(): group_rows = lax.all_gather(owned_rows, 'grp', axis=1, tiled=True)  10.6 us
    ppermute x8, starting transfers between devices, from_behind(): lax.ppermute(shard, axis, [(i, (i + by) % count) for i in range(count)])  6.93 us
    unnamed x20, local copies, waits for them, and re-layouts  4.56 us
  transfers between devices with their start and end apart: 9, of which 9 were waited for; matrix products, arithmetic and copies ran while one was open for 3% of the time, Pallas kernels for 0%

commit v1 on v0

--- a/solution.py
+++ b/solution.py
@@ -5,6 +5,14 @@
 from jax.sharding import PartitionSpec as P
 
 SOFTENING = 0.0001
+
+
+def wait_the_ratios(packet, along_dim):
+    packet = jnp.moveaxis(packet, 0, along_dim)
+    k_now = packet.shape
+    return packet.reshape(
+        *k_now[:along_dim], k_now[along_dim] * k_now[along_dim + 1], *k_now[along_dim + 2 :]
+    )
 
 
 def from_behind(shard, axis, by):
@@ -48,7 +56,28 @@
     device = lax.axis_index("blk") * lax.axis_size("grp") + lax.axis_index("grp")
     offsets = active_index - device * stars_here
     owned_rows = jnp.take(predicted, offsets, axis=1)
-    group_rows = lax.all_gather(owned_rows, "grp", axis=1, tiled=True)
+    nd = lax.axis_size("grp")
+    frames = []
+    m = 0
+    while m < nd:
+        frames.append((m, (m + 1) % nd))
+        m = m + 1
+    seen = []
+    for src_i, u in frames:
+        seen.append((u, src_i))
+    v_now, answer = ([], [])
+    q = 0
+    while q < nd - 1:
+        if q % 2 == 0:
+            v_now.append(lax.ppermute(v_now[-1] if v_now else owned_rows, "grp", perm=frames))
+        else:
+            answer.append(lax.ppermute(answer[-1] if answer else owned_rows, "grp", seen))
+        q = q + 1
+    y = jnp.stack([*v_now[::-1], owned_rows, *answer])
+    small = lax.axis_index("grp")
+    placed = small - len(v_now)
+    y = y[(jnp.arange(nd) - placed) % nd]
+    group_rows = wait_the_ratios(y, 1)
 
     def circulate(number, carry):
         visitor, partial_value = carry

time: 90.2 us -> 98.4 us (1.091)
  blocking collectives: 10.6 us -> 0 us
  starting transfers between devices: 6.96 us -> 16.4 us
  waiting for transfers between devices: 48.9 us -> 56.4 us
  local copies, waits for them, and re-layouts: 6.22 us -> 7.35 us
    all_gather x1 -> x0, blocking collectives: 10.6 us -> none  [local(): group_rows = lax.all_gather(owned_rows, 'grp', axis=1, tiled=True)]
    ppermute x0 -> x7, starting transfers between devices: none -> 8.68 us  [the longest x3 8.18 us: local(): lax.ppermute(answer[-1] if answer else owned_rows, 'grp', seen)]
    ppermute x0 -> x7, waiting for transfers between devices: none -> 7.36 us  [the longest x4 7.26 us: local(): lax.ppermute(v_now[-1] if v_now else owned_rows, 'grp', perm=frames)]
    unnamed x20 -> x23, local copies, waits for them, and re-layouts: 4.56 us -> 4.51 us
  transfers between devices with their start and end apart: 9 -> 16, of which waited for: 9 -> 14; matrix products, arithmetic and copies ran while one was open for 3% -> 3% of each run, Pallas kernels for 0% -> 0%
where the time goes in v1:
time: 98.4 us; the launch traced here: 98 us
  waiting for transfers between devices  56.4 us (57%)
  starting transfers between devices  16.4 us (17%)
  between operations  14.2 us (14%)
  local copies, waits for them, and re-layouts  7.35 us (7%)
  other arithmetic  3.67 us (4%)
    unnamed x2, waiting for transfers between devices  32.5 us
    ppermute x8, waiting for transfers between devices, from_behind(): lax.ppermute(shard, axis, [(i, (i + by) % count) for i in range(count)])  16.5 us
    ppermute x3, starting transfers between devices, local(): lax.ppermute(answer[-1] if answer else owned_rows, 'grp', seen)  8.18 us
    ppermute x8, starting transfers between devices, from_behind(): lax.ppermute(shard, axis, [(i, (i + by) % count) for i in range(count)])  7.68 us
    ppermute x4, waiting for transfers between devices, local(): lax.ppermute(v_now[-1] if v_now else owned_rows, 'grp', perm=frames)  7.26 us
    unnamed x23, local copies, waits for them, and re-layouts  4.51 us
  transfers between devices with their start and end apart: 16, of which 14 were waited for; matrix products, arithmetic and copies ran while one was open for 3% of the time, Pallas kernels for 0%

profile of v1, /device:TPU:0, one launch (start us, length us, event | category | flops | bytes accessed | tf_op | source)
XLA Modules:
  0.0 98.0 jit_solution(16678820844369142173)
XLA Ops:
  7.2 0.0 reduce-scatter.4.cloned.1.call-start
  7.2 0.6 copy-done.6
  7.9 0.0 copy-start.3
  7.9 0.7 copy-done.2
  8.6 0.0 copy-done.3
  8.6 0.7 multiply_add_fusion.1
  9.3 0.0 copy-start
  9.3 0.1 copy.67
  9.5 0.4 copy-done
  9.9 0.6 gather_fusion
  10.5 0.1 broadcast_select_fusion
  10.6 0.5 collective-permute-start.2
  11.1 2.9 %collective-permute-start.6 = (f32[6,16]{0,1:T(8,128)S(1)}, f32[6,16]{0,1:T(8,128)S(1)}, u32[]{:S(2)}, u32[]{:S(2)}) collective-permute-start(f32[6,16]{0,1:T(8,128)S(1)} %broadcast_select_fusion), channel_id=1, source_target_pairs={{1,0},{2,1},{3,2},{4,3},{5,4},{6,5},{7,6},{0,7},{9,8},{10,9},{11,1... | collective-permute-start | bytes 1160 | tf_op jit(solution)/shard_map/ppermute | solution.py:74
  14.0 1.3 %collective-permute-done.2 = f32[6,16]{0,1:T(8,128)S(1)} collective-permute-done((f32[6,16]{0,1:T(8,128)S(1)}, f32[6,16]{0,1:T(8,128)S(1)}, u32[]{:S(2)}, u32[]{:S(2)}) %collective-permute-start.2) | collective-permute-done | bytes 416 | tf_op jit(solution)/shard_map/ppermute | solution.py:72
  15.3 0.1 collective-permute-done.6
  15.4 2.6 %collective-permute-start.7 = (f32[6,16]{0,1:T(8,128)S(1)}, f32[6,16]{0,1:T(8,128)S(1)}, u32[]{:S(2)}, u32[]{:S(2)}) collective-permute-start(f32[6,16]{0,1:T(8,128)S(1)} %collective-permute-done.6), channel_id=1, source_target_pairs={{1,0},{2,1},{3,2},{4,3},{5,4},{6,5},{7,6},{0,7},{9,8},{10,9},{11,1... | collective-permute-start | bytes 1160 | tf_op jit(solution)/shard_map/ppermute | solution.py:74
  18.0 1.3 %collective-permute-done.3 = f32[6,16]{0,1:T(8,128)S(1)} collective-permute-done((f32[6,16]{0,1:T(8,128)S(1)}, f32[6,16]{0,1:T(8,128)S(1)}, u32[]{:S(2)}, u32[]{:S(2)}) %collective-permute-start.3) | collective-permute-done | bytes 416 | tf_op jit(solution)/shard_map/ppermute | solution.py:72
  19.3 0.1 copy.72
  19.3 0.0 collective-permute-done.7
  19.4 2.6 %collective-permute-start.8 = (f32[6,16]{0,1:T(8,128)S(1)}, f32[6,16]{0,1:T(8,128)S(1)}, u32[]{:S(2)}, u32[]{:S(2)}) collective-permute-start(f32[6,16]{0,1:T(8,128)S(1)} %collective-permute-done.7), channel_id=1, source_target_pairs={{1,0},{2,1},{3,2},{4,3},{5,4},{6,5},{7,6},{0,7},{9,8},{10,9},{11,1... | collective-permute-start | bytes 1160 | tf_op jit(solution)/shard_map/ppermute | solution.py:74
  22.0 1.2 %collective-permute-done.4 = f32[6,16]{0,1:T(8,128)S(1)} collective-permute-done((f32[6,16]{0,1:T(8,128)S(1)}, f32[6,16]{0,1:T(8,128)S(1)}, u32[]{:S(2)}, u32[]{:S(2)}) %collective-permute-start.4) | collective-permute-done | bytes 416 | tf_op jit(solution)/shard_map/ppermute | solution.py:72
  23.2 0.1 copy.73
  23.3 0.1 copy.71
  23.4 0.1 copy.74
  23.5 0.1 copy.70
  23.5 0.1 copy.69
  23.6 0.1 copy.75
  23.7 3.5 %collective-permute-done.5 = f32[6,16]{0,1:T(8,128)S(1)} collective-permute-done((f32[6,16]{0,1:T(8,128)S(1)}, f32[6,16]{0,1:T(8,128)S(1)}, u32[]{:S(2)}, u32[]{:S(2)}) %collective-permute-start.5) | collective-permute-done | bytes 416 | tf_op jit(solution)/shard_map/ppermute | solution.py:72
  27.2 0.1 copy.68
  27.3 0.6 gather_fusion.1
  27.9 0.1 reshape.135
  28.0 0.7 copy-done.1
  28.7 27.1 %while.11 = (s32[]{:T(128)}, f32[6,128]{1,0:T(8,128)S(1)}, f32[6,128]{1,0:T(8,128)S(1)}, f32[3,512]{1,0:T(4,128)S(1)}, f32[512]{0:T(512)S(1)}, /*index=5*/f32[3,512]{1,0:T(4,128)S(1)}, s32[]{:T(128)}) while((s32[]{:T(128)}, f32[6,128]{1,0:T(8,128)S(1)}, f32[6,128]{1,0:T(8,128)S(1)}, f32[3,512]{1,0:T(4,128)S(1)}, f32[512]{0:T(512)S(1)}, ...), condition=%wide.region_5.6_spmd, body=%wide.region_0.5_spmd.sunk | while | flops 3015426 | bytes 2179229 | solution.py:88
  28.7 2.3 %collective-permute-start = (f32[6,128]{1,0:T(8,128)S(1)}, f32[6,128]{1,0:T(8,128)S(1)}, u32[]{:S(2)}, u32[]{:S(2)}) collective-permute-start(f32[6,128]{1,0:T(8,128)S(1)} %copy.92), channel_id=1, source_target_pairs={{0,8},{8,16},{16,24},{24,0},{1,9},{9,17},{17,25},{25,1},{2,10},{10... | collective-permute-start | bytes 9224 | tf_op jit(solution)/shard_map/while/body/eval_jaxpr/ppermute | solution.py:20
  31.0 0.2 fusion.13
  31.2 0.1 multiply_divide_fusion.2
  31.3 0.4 fusion.14
  31.7 1.6 %collective-permute-start.1 = (f32[6,128]{1,0:T(8,128)S(1)}, f32[6,128]{1,0:T(8,128)S(1)}, u32[]{:S(2)}, u32[]{:S(2)}) collective-permute-start(f32[6,128]{1,0:T(8,128)S(1)} %maximum_add_fusion.2), channel_id=1, source_target_pairs={{0,8},{8,16},{16,24},{24,0},{1,9},{9,17},{17,25},{25,1},{2,10},{10... | collective-permute-start | bytes 9224 | tf_op jit(solution)/shard_map/while/body/eval_jaxpr/ppermute | solution.py:20
  33.4 1.2 %collective-permute-done = f32[6,128]{1,0:T(8,128)S(1)} collective-permute-done((f32[6,128]{1,0:T(8,128)S(1)}, f32[6,128]{1,0:T(8,128)S(1)}, u32[]{:S(2)}, u32[]{:S(2)}) %collective-permute-start) | collective-permute-done | bytes 3104 | tf_op jit(solution)/shard_map/while/body/eval_jaxpr/ppermute | solution.py:20
  34.6 2.6 %collective-permute-done.1 = f32[6,128]{1,0:T(8,128)S(1)} collective-permute-done((f32[6,128]{1,0:T(8,128)S(1)}, f32[6,128]{1,0:T(8,128)S(1)}, u32[]{:S(2)}, u32[]{:S(2)}) %collective-permute-start.1) | collective-permute-done | bytes 3104 | tf_op jit(solution)/shard_map/while/body/eval_jaxpr/ppermute | solution.py:20
  37.2 0.2 fusion.13
  37.4 0.1 multiply_divide_fusion.2
  37.5 0.4 fusion.14
  37.9 1.4 %collective-permute-start.1 = (f32[6,128]{1,0:T(8,128)S(1)}, f32[6,128]{1,0:T(8,128)S(1)}, u32[]{:S(2)}, u32[]{:S(2)}) collective-permute-start(f32[6,128]{1,0:T(8,128)S(1)} %maximum_add_fusion.2), channel_id=1, source_target_pairs={{0,8},{8,16},{16,24},{24,0},{1,9},{9,17},{17,25},{25,1},{2,10},{10... | collective-permute-start | bytes 9224 | tf_op jit(solution)/shard_map/while/body/eval_jaxpr/ppermute | solution.py:20
  39.3 3.3 %collective-permute-done = f32[6,128]{1,0:T(8,128)S(1)} collective-permute-done((f32[6,128]{1,0:T(8,128)S(1)}, f32[6,128]{1,0:T(8,128)S(1)}, u32[]{:S(2)}, u32[]{:S(2)}) %collective-permute-start) | collective-permute-done | bytes 3104 | tf_op jit(solution)/shard_map/while/body/eval_jaxpr/ppermute | solution.py:20
  42.6 0.8 collective-permute-done.1
  43.4 0.2 fusion.13
  43.6 0.1 multiply_divide_fusion.2
  43.7 0.4 fusion.14
  44.1 0.9 collective-permute-start.1
  45.0 3.8 %collective-permute-done = f32[6,128]{1,0:T(8,128)S(1)} collective-permute-done((f32[6,128]{1,0:T(8,128)S(1)}, f32[6,128]{1,0:T(8,128)S(1)}, u32[]{:S(2)}, u32[]{:S(2)}) %collective-permute-start) | collective-permute-done | bytes 3104 | tf_op jit(solution)/shard_map/while/body/eval_jaxpr/ppermute | solution.py:20
  48.8 0.8 collective-permute-done.1
  49.6 0.2 fusion.13
  49.8 0.1 multiply_divide_fusion.2
  49.9 0.4 fusion.14
  50.3 1.4 %collective-permute-start.1 = (f32[6,128]{1,0:T(8,128)S(1)}, f32[6,128]{1,0:T(8,128)S(1)}, u32[]{:S(2)}, u32[]{:S(2)}) collective-permute-start(f32[6,128]{1,0:T(8,128)S(1)} %maximum_add_fusion.2), channel_id=1, source_target_pairs={{0,8},{8,16},{16,24},{24,0},{1,9},{9,17},{17,25},{25,1},{2,10},{10... | collective-permute-start | bytes 9224 | tf_op jit(solution)/shard_map/while/body/eval_jaxpr/ppermute | solution.py:20
  51.7 3.3 %collective-permute-done = f32[6,128]{1,0:T(8,128)S(1)} collective-permute-done((f32[6,128]{1,0:T(8,128)S(1)}, f32[6,128]{1,0:T(8,128)S(1)}, u32[]{:S(2)}, u32[]{:S(2)}) %collective-permute-start) | collective-permute-done | bytes 3104 | tf_op jit(solution)/shard_map/while/body/eval_jaxpr/ppermute | solution.py:20
  55.0 0.8 collective-permute-done.1
  55.8 0.7 copy.77
  56.5 0.0 reduce-scatter.4.cloned.1.call-update
  56.5 32.5 %reduce-scatter.4.cloned.1.call-done = f32[16,6]{1,0:T(8,128)} async-done(((f32[128,6]{1,0:T(8,128)}), f32[16,6]{1,0:T(8,128)}) %reduce-scatter.4.cloned.1.call-update) | async-done | bytes 400
  89.0 0.8 fusion.8
  89.9 0.7 copy.80
  90.5 0.7 copy.79
  (42 shorter events, 0.2 us)
Async XLA Ops:
  7.2 81.9 %reduce-scatter.4.cloned.1.call-start = ((), (), s32[]{:S(2)}) async-start(), calls=%async_computation.1 | async-start | bytes 73728
  7.2 1.4 %copy-start.5 = (f32[3,512]{1,0:T(4,128)S(1)}, f32[3,512]{1,0:T(4,128)}, u32[]{:S(2)}) copy-start(f32[3,512]{1,0:T(4,128)} %param.9) | copy-start | bytes 18436
  7.2 0.7 copy-start.6
  7.2 1.4 %copy-start.4 = (f32[3,512]{1,0:T(4,128)S(1)}, f32[3,512]{1,0:T(4,128)}, u32[]{:S(2)}) copy-start(f32[3,512]{1,0:T(4,128)} %param.11) | copy-start | bytes 18436
  7.9 0.7 copy-start.2
  7.9 0.7 copy-start.3
  9.3 0.6 copy-start
  10.6 4.7 %collective-permute-start.2 = (f32[6,16]{0,1:T(8,128)S(1)}, f32[6,16]{0,1:T(8,128)S(1)}, u32[]{:S(2)}, u32[]{:S(2)}) collective-permute-start(f32[6,16]{0,1:T(8,128)S(1)} %broadcast_select_fusion), channel_id=1, source_target_pairs={{0,1},{1,2},{2,3},{3,4},{4,5},{5,6},{6,7},{7,0},{8,9},{9,10},{10,1... | collective-permute-start | bytes 1160 | tf_op jit(solution)/shard_map/ppermute | solution.py:72
  11.1 4.3 %collective-permute-start.6 = (f32[6,16]{0,1:T(8,128)S(1)}, f32[6,16]{0,1:T(8,128)S(1)}, u32[]{:S(2)}, u32[]{:S(2)}) collective-permute-start(f32[6,16]{0,1:T(8,128)S(1)} %broadcast_select_fusion), channel_id=1, source_target_pairs={{1,0},{2,1},{3,2},{4,3},{5,4},{6,5},{7,6},{0,7},{9,8},{10,9},{11,1... | collective-permute-start | bytes 1160 | tf_op jit(solution)/shard_map/ppermute | solution.py:74
  15.3 4.0 %collective-permute-start.3 = (f32[6,16]{0,1:T(8,128)S(1)}, f32[6,16]{0,1:T(8,128)S(1)}, u32[]{:S(2)}, u32[]{:S(2)}) collective-permute-start(f32[6,16]{0,1:T(8,128)S(1)} %collective-permute-done.2), channel_id=1, source_target_pairs={{0,1},{1,2},{2,3},{3,4},{4,5},{5,6},{6,7},{7,0},{8,9},{9,10},{10,1... | collective-permute-start | bytes 1160 | tf_op jit(solution)/shard_map/ppermute | solution.py:72
  15.4 4.0 %collective-permute-start.7 = (f32[6,16]{0,1:T(8,128)S(1)}, f32[6,16]{0,1:T(8,128)S(1)}, u32[]{:S(2)}, u32[]{:S(2)}) collective-permute-start(f32[6,16]{0,1:T(8,128)S(1)} %collective-permute-done.6), channel_id=1, source_target_pairs={{1,0},{2,1},{3,2},{4,3},{5,4},{6,5},{7,6},{0,7},{9,8},{10,9},{11,1... | collective-permute-start | bytes 1160 | tf_op jit(solution)/shard_map/ppermute | solution.py:74
  19.3 4.0 %collective-permute-start.4 = (f32[6,16]{0,1:T(8,128)S(1)}, f32[6,16]{0,1:T(8,128)S(1)}, u32[]{:S(2)}, u32[]{:S(2)}) collective-permute-start(f32[6,16]{0,1:T(8,128)S(1)} %collective-permute-done.3), channel_id=1, source_target_pairs={{0,1},{1,2},{2,3},{3,4},{4,5},{5,6},{6,7},{7,0},{8,9},{9,10},{10,1... | collective-permute-start | bytes 1160 | tf_op jit(solution)/shard_map/ppermute | solution.py:72
  19.4 4.3 %collective-permute-start.8 = (f32[6,16]{0,1:T(8,128)S(1)}, f32[6,16]{0,1:T(8,128)S(1)}, u32[]{:S(2)}, u32[]{:S(2)}) collective-permute-start(f32[6,16]{0,1:T(8,128)S(1)} %collective-permute-done.7), channel_id=1, source_target_pairs={{1,0},{2,1},{3,2},{4,3},{5,4},{6,5},{7,6},{0,7},{9,8},{10,9},{11,1... | collective-permute-start | bytes 1160 | tf_op jit(solution)/shard_map/ppermute | solution.py:74
  23.2 4.0 %collective-permute-start.5 = (f32[6,16]{0,1:T(8,128)S(1)}, f32[6,16]{0,1:T(8,128)S(1)}, u32[]{:S(2)}, u32[]{:S(2)}) collective-permute-start(f32[6,16]{0,1:T(8,128)S(1)} %collective-permute-done.4), channel_id=1, source_target_pairs={{0,1},{1,2},{2,3},{3,4},{4,5},{5,6},{6,7},{7,0},{8,9},{9,10},{10,1... | collective-permute-start | bytes 1160 | tf_op jit(solution)/shard_map/ppermute | solution.py:72
  28.0 0.7 copy-start.1
  28.7 5.9 %collective-permute-start = (f32[6,128]{1,0:T(8,128)S(1)}, f32[6,128]{1,0:T(8,128)S(1)}, u32[]{:S(2)}, u32[]{:S(2)}) collective-permute-start(f32[6,128]{1,0:T(8,128)S(1)} %copy.92), channel_id=1, source_target_pairs={{0,8},{8,16},{16,24},{24,0},{1,9},{9,17},{17,25},{25,1},{2,10},{10... | collective-permute-start | bytes 9224 | tf_op jit(solution)/shard_map/while/body/eval_jaxpr/ppermute | solution.py:20
  31.7 5.5 %collective-permute-start.1 = (f32[6,128]{1,0:T(8,128)S(1)}, f32[6,128]{1,0:T(8,128)S(1)}, u32[]{:S(2)}, u32[]{:S(2)}) collective-permute-start(f32[6,128]{1,0:T(8,128)S(1)} %maximum_add_fusion.2), channel_id=1, source_target_pairs={{0,8},{8,16},{16,24},{24,0},{1,9},{9,17},{17,25},{25,1},{2,10},{10... | collective-permute-start | bytes 9224 | tf_op jit(solution)/shard_map/while/body/eval_jaxpr/ppermute | solution.py:20
  37.2 5.4 %collective-permute-start = (f32[6,128]{1,0:T(8,128)S(1)}, f32[6,128]{1,0:T(8,128)S(1)}, u32[]{:S(2)}, u32[]{:S(2)}) collective-permute-start(f32[6,128]{1,0:T(8,128)S(1)} %copy.92), channel_id=1, source_target_pairs={{0,8},{8,16},{16,24},{24,0},{1,9},{9,17},{17,25},{25,1},{2,10},{10... | collective-permute-start | bytes 9224 | tf_op jit(solution)/shard_map/while/body/eval_jaxpr/ppermute | solution.py:20
  37.9 5.5 %collective-permute-start.1 = (f32[6,128]{1,0:T(8,128)S(1)}, f32[6,128]{1,0:T(8,128)S(1)}, u32[]{:S(2)}, u32[]{:S(2)}) collective-permute-start(f32[6,128]{1,0:T(8,128)S(1)} %maximum_add_fusion.2), channel_id=1, source_target_pairs={{0,8},{8,16},{16,24},{24,0},{1,9},{9,17},{17,25},{25,1},{2,10},{10... | collective-permute-start | bytes 9224 | tf_op jit(solution)/shard_map/while/body/eval_jaxpr/ppermute | solution.py:20
  43.4 5.4 %collective-permute-start = (f32[6,128]{1,0:T(8,128)S(1)}, f32[6,128]{1,0:T(8,128)S(1)}, u32[]{:S(2)}, u32[]{:S(2)}) collective-permute-start(f32[6,128]{1,0:T(8,128)S(1)} %copy.92), channel_id=1, source_target_pairs={{0,8},{8,16},{16,24},{24,0},{1,9},{9,17},{17,25},{25,1},{2,10},{10... | collective-permute-start | bytes 9224 | tf_op jit(solution)/shard_map/while/body/eval_jaxpr/ppermute | solution.py:20
  44.1 5.5 %collective-permute-start.1 = (f32[6,128]{1,0:T(8,128)S(1)}, f32[6,128]{1,0:T(8,128)S(1)}, u32[]{:S(2)}, u32[]{:S(2)}) collective-permute-start(f32[6,128]{1,0:T(8,128)S(1)} %maximum_add_fusion.2), channel_id=1, source_target_pairs={{0,8},{8,16},{16,24},{24,0},{1,9},{9,17},{17,25},{25,1},{2,10},{10... | collective-permute-start | bytes 9224 | tf_op jit(solution)/shard_map/while/body/eval_jaxpr/ppermute | solution.py:20
  49.6 5.4 %collective-permute-start = (f32[6,128]{1,0:T(8,128)S(1)}, f32[6,128]{1,0:T(8,128)S(1)}, u32[]{:S(2)}, u32[]{:S(2)}) collective-permute-start(f32[6,128]{1,0:T(8,128)S(1)} %copy.92), channel_id=1, source_target_pairs={{0,8},{8,16},{16,24},{24,0},{1,9},{9,17},{17,25},{25,1},{2,10},{10... | collective-permute-start | bytes 9224 | tf_op jit(solution)/shard_map/while/body/eval_jaxpr/ppermute | solution.py:20
  50.3 5.5 %collective-permute-start.1 = (f32[6,128]{1,0:T(8,128)S(1)}, f32[6,128]{1,0:T(8,128)S(1)}, u32[]{:S(2)}, u32[]{:S(2)}) collective-permute-start(f32[6,128]{1,0:T(8,128)S(1)} %maximum_add_fusion.2), channel_id=1, source_target_pairs={{0,8},{8,16},{16,24},{24,0},{1,9},{9,17},{17,25},{25,1},{2,10},{10... | collective-permute-start | bytes 9224 | tf_op jit(solution)/shard_map/while/body/eval_jaxpr/ppermute | solution.py:20
Sparse Core Ops, SparseCore 0:
  56.7 32.3 reduce-scatter.3
